TPU v7x, 32 devices: a whole 2x2x4 slice. The times are simulated.
32 devices in a mesh: member: 4 (over x, core), tile: 4 (over z), grp: 2 (over y).
Axes of the slice: x: 2, y: 2, z: 4, core: 2. Of those that a mesh axis runs over, the one named last changes fastest.
Arguments:
- members: float32 [80, 128, 1024], P(('member', 'grp'), 'tile'), may hold values from -6 to 6
- courant_x: float32 [128, 1024], P('tile'), may hold values from -0.48 to 0.48
- courant_y: float32 [128, 1024], P('tile'), may hold values from -0.48 to 0.48
- obs_cell: int32 [4, 8, 1024], P('tile', ('member', 'grp')), may hold values from 0 to 4095
- innovation: float32 [4, 8, 1024], P('tile', ('member', 'grp')), may hold values from -6 to 6
- obs_weight: float32 [4, 8, 1024], P('tile', ('member', 'grp')), may hold values from 0.5 to 3
- stencil_offsets: int32 [9, 2], replicated, may hold values from -2 to 2, as said below
- stencil_weights: float32 [9], replicated, may hold values from 0.2 to 1
Outputs:
- analysis: float32 [80, 128, 1024], P(('member', 'grp'), 'tile')
- increment: float32 [128, 1024], P('tile', ('member', 'grp'))
Inputs may be any that keep to these rules, and one draw needn't show every extreme that they name: `stencil_offsets`: each row is a stencil entry's offsets along rows and columns; some entry reaches 2 cells along rows and some along columns. `obs_cell`: cells of a block are numbered row by row, 128 to a row.
All inputs are finite; a program needn't handle non-finite values.
Results may differ from a plain program's by a relative error of at most 0.0001.
Values sent between devices are 32-bit elements; how exact they have to be, the bound alone decides.
A program may use at most 128 MiB of HBM per device.

v0:
```python
import math
import jax
import jax.numpy as jnp
from jax import lax
from jax.sharding import PartitionSpec as P

RADIUS = 2
FSTEPS = 3
STEP_SIZE = 0.25
GROUP = ("member", "grp")


def halo(cells, axis, width, dim):
    count = lax.axis_size(axis)
    head = lax.slice_in_dim(cells, 0, width, axis=dim)
    tail = lax.slice_in_dim(cells, cells.shape[dim] - width, cells.shape[dim], axis=dim)
    above = lax.ppermute(tail, axis, [(i, i + 1) for i in range(count - 1)])
    below = lax.ppermute(head, axis, [(i + 1, i) for i in range(count - 1)])
    return jnp.concatenate([above, cells, below], axis=dim)


def upwind(q, cx, cy):
    rows = q.shape[1]
    c = q[:, 1:-1]
    left = jnp.pad(c, ((0, 0), (0, 0), (1, 0)))[:, :, :-1]
    right = jnp.pad(c, ((0, 0), (0, 0), (0, 1)))[:, :, 1:]
    return (
        c
        - jnp.maximum(cx, 0.0) * (c - q[:, : rows - 2])
        - jnp.minimum(cx, 0.0) * (q[:, 2:] - c)
        - jnp.maximum(cy, 0.0) * (c - left)
        - jnp.minimum(cy, 0.0) * (right - c)
    )


def spread_out(f, taps, sign):
    rows = f.shape[1] - 2 * RADIUS
    cols = f.shape[2]
    g = jnp.pad(f, ((0, 0), (0, 0), (RADIUS, RADIUS)))
    total = 0.0
    for r in range(-RADIUS, RADIUS + 1):
        for c in range(-RADIUS, RADIUS + 1):
            part = g[
                :,
                RADIUS + sign * r : RADIUS + sign * r + rows,
                RADIUS + sign * c : RADIUS + sign * c + cols,
            ]
            total = total + taps[r + RADIUS, c + RADIUS] * part
    return total


def on_device(members, courant_x, courant_y, obs_cell, innovation, obs_weight, offsets, weights):
    n, rows, cols = members.shape
    reach = 2 * RADIUS
    edge = reach + FSTEPS
    groups = lax.axis_size(GROUP)
    total = n * groups
    tile = lax.axis_index("tile")
    tiles = lax.axis_size("tile")
    packed = halo(jnp.concatenate([members, courant_x[None], courant_y[None]]), "tile", edge, 1)
    q, cx, cy = (packed[:n], packed[n], packed[n + 1])
    for s in range(FSTEPS):
        lo, hi = (s + 1, rows + 2 * edge - s - 1)
        q = upwind(q, cx[lo:hi], cy[lo:hi])
    fields = q[:, reach : reach + rows]
    own = jnp.sum(q, axis=0) / n
    mean = lax.psum(own, GROUP) / groups
    dev = (q - own[None]) / math.sqrt(total - 1)
    shift = (own - mean) * math.sqrt(n / (total - 1))
    ones = jnp.full_like(own, 1.0 / math.sqrt(groups))
    dev = jnp.concatenate([dev, shift[None], ones[None]])
    kr = jnp.arange(-RADIUS, RADIUS + 1)
    hit = (offsets[:, 0][:, None, None] == kr[None, :, None]) & (
        offsets[:, 1][:, None, None] == kr[None, None, :]
    )
    taps = jnp.sum(jnp.where(hit, weights[:, None, None], 0.0), axis=0) / jnp.sum(weights)
    at = jnp.arange(rows + 2 * RADIUS) - RADIUS + tile * rows
    inside = ((at >= 0) & (at < tiles * rows)).astype(jnp.float32)[None, :, None]

    def apply(h):
        z = spread_out(dev * h[None], taps, -1) * inside
        y = spread_out(z, taps, 1)
        return jnp.sum(dev[:, reach : reach + rows] * y, axis=0) * -STEP_SIZE

    width = cols // groups
    cell = obs_cell.reshape(-1)
    w = obs_weight.reshape(-1)
    wi = w * innovation.reshape(-1)
    pick_r = (cell[None] // width == jnp.arange(rows)[:, None]).astype(jnp.float32)
    pick_c = (cell[:, None] % width == jnp.arange(width)[None]).astype(jnp.float32)
    both = jnp.dot(
        jnp.concatenate([pick_r * w[None], pick_r * wi[None]]),
        pick_c,
        precision=lax.Precision.HIGHEST,
    )
    dense_w, dense_wi = (both[:rows], both[rows:])

    def gathered(block):
        return halo(lax.all_gather(block, GROUP, axis=1, tiled=True), "tile", reach, 0)

    x0 = lax.psum_scatter(apply(gathered(-dense_wi)), GROUP, scatter_dimension=1, tiled=True)
    g1 = dense_w * x0 - dense_wi
    x1 = lax.psum_scatter(apply(gathered(g1)), GROUP, scatter_dimension=1, tiled=True)
    block = (1.0 - STEP_SIZE) * x0 + x1
    full = lax.all_gather(block, GROUP, axis=1, tiled=True)
    return (fields + full[None], block)


def solution(mesh):
    placed = (
        P(GROUP, "tile", None),
        P("tile", None),
        P("tile", None),
        P("tile", GROUP, None),
        P("tile", GROUP, None),
        P("tile", GROUP, None),
        P(),
        P(),
    )
    return jax.shard_map(
        on_device,
        mesh=mesh,
        in_specs=placed,
        out_specs=(P(GROUP, "tile", None), P("tile", GROUP)),
        check_vma=False,
    )
```

profile of v0, /device:TPU:1, one launch (start us, length us, event | category | flops | bytes accessed | tf_op | source)
XLA Modules:
  0.0 334.2 jit_solution(7404053742297085599)
XLA Ops:
  7.2 0.8 add_select_fusion
  8.0 0.7 mul.748
  8.7 0.7 fusion.218
  9.4 0.4 fusion.212
  9.9 15.2 %all_gather.9 = f32[32,1024]{1,0:T(8,128)S(1)} all-gather(f32[32,128]{1,0:T(8,128)S(1)} %slice_negate_fusion), channel_id=1, replica_groups=mesh['member'=4,'tile'=4,'grp'=2] {'member','grp'}, dimensions={1}, use_global_device_ids=true | all-gather | bytes 147456 | tf_op jit(solution)/shard_map/all_gather | solution.py:99
  25.1 0.7 copy-done.7
  25.8 3.2 collective-permute-start.2
  29.0 1.3 collective-permute-start.3
  30.3 1.2 pad_maximum_fusion.3
  31.5 4.0 %collective-permute-start = (f32[12,7,1024]{2,1,0:T(8,128)S(1)}, f32[12,7,1024]{2,1,0:T(8,128)S(1)}, u32[]{:S(2)}, u32[]{:S(2)}) collective-permute-start(f32[12,7,1024]{2,1,0:T(8,128)S(1)} %get-tuple-element.24), channel_id=1, source_target_pairs={{0,2},{2,4},{4,6},{1,3},{3,5},{5,7},{8,10},{10,12},{12,14},{9,11},... | collective-permute-start | bytes 1032200 | tf_op jit(solution)/shard_map/ppermute | solution.py:17
  35.5 1.3 collective-permute-start.1
  36.8 0.6 reduce_sum.47
  37.6 0.7 broadcast_divide_fusion
  38.3 0.7 fusion.228
  39.0 0.7 fusion.227
  39.7 4.1 %collective-permute-done = f32[12,7,1024]{2,1,0:T(8,128)S(1)} collective-permute-done((f32[12,7,1024]{2,1,0:T(8,128)S(1)}, f32[12,7,1024]{2,1,0:T(8,128)S(1)}, u32[]{:S(2)}, u32[]{:S(2)}) %collective-permute-start) | collective-permute-done | bytes 344096 | tf_op jit(solution)/shard_map/ppermute | solution.py:17
  43.8 3.9 %collective-permute-done.1 = f32[12,7,1024]{2,1,0:T(8,128)S(1)} collective-permute-done((f32[12,7,1024]{2,1,0:T(8,128)S(1)}, f32[12,7,1024]{2,1,0:T(8,128)S(1)}, u32[]{:S(2)}, u32[]{:S(2)}) %collective-permute-start.1) | collective-permute-done | bytes 344096 | tf_op jit(solution)/shard_map/ppermute | solution.py:18
  47.7 0.3 pad_maximum_fusion
  48.0 0.4 slice.749
  48.5 1.5 fusion.93
  50.0 0.4 slice.752
  50.6 1.5 fusion.99
  52.5 1.1 fusion.223
  53.6 0.6 copy-done.6
  54.3 0.3 subtract_multiply_fusion
  54.7 0.3 copy-done.5
  54.9 0.4 all-reduce.12.cloned.1.call-update
  55.6 0.9 pad_maximum_fusion.10
  56.5 55.5 %all-reduce.12.cloned.1.call-done = f32[40,1024]{1,0:T(8,128)} async-done(((f32[40,1024]{1,0:T(8,128)}), f32[40,1024]{1,0:T(8,128)}) %all-reduce.12.cloned.1.call-update) | async-done | bytes 163856 | tf_op jit(solution)/shard_map/psum | solution.py:67
  112.0 1.0 multiply_bitcast_fusion
  113.1 1.7 maximum_maximum_fusion
  114.7 26.1 %fusion.44 = f32[12,36,1024]{2,1,0:T(8,128)S(1)} fusion(f32[12,40,1024]{2,1,0:T(8,128)S(1)} %get-tuple-element.23, f32[36]{0:T(128)S(1)} %and_convert_fusion, f32[]{:T(128)} %bitcast.44, f32[]{:T(128)} %bitcast.43, f32[]{:T(128)} %bitcast.42, f32[]{:T(128)} %bitcast.41, f32[]{:T(128)} %bitcast.40, f32[]{:T(128)} %bitcast.39, f32[]{:T(128)} %bitcast.38, ...), kind=kLoop, calls=%fused_computation.129 | loop fusion | flops 22118400 | bytes 13566564 | tf_op jit(solution)/shard_map/mul | solution.py:81
  140.9 25.1 %fusion.164 = f32[32,1024]{1,0:T(8,128)S(1)} fusion(f32[12,36,1024]{2,1,0:T(8,128)S(1)} %fusion.44, f32[12,40,1024]{2,1,0:T(8,128)} %get-tuple-element.22, f32[]{:T(128)} %bitcast.44, f32[]{:T(128)} %bitcast.43, f32[]{:T(128)} %bitcast.42, f32[]{:T(128)} %bitcast.41, f32[]{:T(128)} %bitcast.40, f32[]{:T(128)} %bitcast.39, f32[]{:T(128)} %bitcast.38, ...), kind=kLoop, calls=%fused_computation.269 | loop fusion | flops 20021248 | bytes 11534436 | tf_op jit(solution)/shard_map/reduce_sum | solution.py:83
  165.9 0.7 broadcast_multiply_fusion.4
  166.7 33.3 %reduce-scatter.3.cloned.1.call-done = f32[32,128]{1,0:T(8,128)} async-done(((f32[32,1024]{1,0:T(8,128)}), f32[32,128]{1,0:T(8,128)}) %reduce-scatter.3.cloned.1.call-update) | async-done | bytes 16400 | tf_op jit(solution)/shard_map/reduce_scatter | solution.py:101
  200.0 0.7 fusion.219
  200.7 14.9 %all_gather.10 = f32[32,1024]{1,0:T(8,128)S(1)} all-gather(f32[32,128]{1,0:T(8,128)S(1)} %fusion.219), channel_id=1, replica_groups=mesh['member'=4,'tile'=4,'grp'=2] {'member','grp'}, dimensions={1}, use_global_device_ids=true | all-gather | bytes 147456 | tf_op jit(solution)/shard_map/all_gather | solution.py:99
  215.6 3.1 collective-permute-start.4
  218.7 1.5 collective-permute-start.5
  220.2 3.4 %collective-permute-done.5 = f32[4,1024]{1,0:T(4,128)S(1)} collective-permute-done((f32[4,1024]{1,0:T(4,128)S(1)}, f32[4,1024]{1,0:T(4,128)S(1)}, u32[]{:S(2)}, u32[]{:S(2)}) %collective-permute-start.5) | collective-permute-done | bytes 16416 | tf_op jit(solution)/shard_map/ppermute | solution.py:18
  223.6 1.7 broadcast_multiply_fusion
  225.4 26.2 %fusion.89 = f32[12,36,1024]{2,1,0:T(8,128)S(1)} fusion(f32[12,40,1024]{2,1,0:T(8,128)S(1)} %broadcast_multiply_fusion, f32[36]{0:T(128)S(1)} %and_convert_fusion, f32[]{:T(128)} %bitcast.44, f32[]{:T(128)} %bitcast.43, f32[]{:T(128)} %bitcast.42, f32[]{:T(128)} %bitcast.41, f32[]{:T(128)} %bitcast.40, f32[]{:T(128)} %bitcast.39, f32[]{:T(128)} %bitcast.38, ...), kind=kLoop, calls=%fused_computation.174 | loop fusion | flops 22118400 | bytes 13566564 | tf_op jit(solution)/shard_map/mul | solution.py:81
  251.5 25.1 %fusion.210 = f32[32,1024]{1,0:T(8,128)S(1)} fusion(f32[12,36,1024]{2,1,0:T(8,128)S(1)} %fusion.89, f32[12,40,1024]{2,1,0:T(8,128)} %get-tuple-element.22, f32[]{:T(128)} %bitcast.44, f32[]{:T(128)} %bitcast.43, f32[]{:T(128)} %bitcast.42, f32[]{:T(128)} %bitcast.41, f32[]{:T(128)} %bitcast.40, f32[]{:T(128)} %bitcast.39, f32[]{:T(128)} %bitcast.38, ...), kind=kLoop, calls=%fused_computation.315 | loop fusion | flops 20021248 | bytes 11534436 | tf_op jit(solution)/shard_map/reduce_sum | solution.py:83
  276.6 0.7 broadcast_multiply_fusion.3
  277.3 32.0 %reduce-scatter.5.cloned.1.call-done = f32[32,128]{1,0:T(8,128)} async-done(((f32[32,1024]{1,0:T(8,128)}), f32[32,128]{1,0:T(8,128)}) %reduce-scatter.5.cloned.1.call-update) | async-done | bytes 16400 | tf_op jit(solution)/shard_map/reduce_scatter | solution.py:103
  309.3 0.7 multiply_add_fusion
  310.0 14.9 %all_gather.11 = f32[32,1024]{1,0:T(8,128)S(1)} all-gather(f32[32,128]{1,0:T(8,128)S(1)} %multiply_add_fusion), channel_id=1, replica_groups=mesh['member'=4,'tile'=4,'grp'=2] {'member','grp'}, dimensions={1}, use_global_device_ids=true | all-gather | bytes 147456 | tf_op jit(solution)/shard_map/all_gather | solution.py:105
  324.9 2.7 slice_add_fusion
  (47 shorter events, 1.3 us)
Async XLA Ops:
  7.2 40.5 %copy-start = (f32[10,32,1024]{2,1,0:T(8,128)S(1)}, f32[10,32,1024]{2,1,0:T(8,128)}, u32[]{:S(2)}) copy-start(f32[10,32,1024]{2,1,0:T(8,128)} %param.8) | copy-start | bytes 3932164
  7.2 40.5 %copy-start.3 = (f32[32,1024]{1,0:T(8,128)S(1)}, f32[32,1024]{1,0:T(8,128)}, u32[]{:S(2)}) copy-start(f32[32,1024]{1,0:T(8,128)} %param.10) | copy-start | bytes 393220
  7.2 40.5 %copy-start.4 = (f32[32,1024]{1,0:T(8,128)S(1)}, f32[32,1024]{1,0:T(8,128)}, u32[]{:S(2)}) copy-start(f32[32,1024]{1,0:T(8,128)} %param.9) | copy-start | bytes 393220
  7.2 29.6 %copy-start.10 = (s32[9,2]{0,1:T(2,128)S(1)}, s32[9,2]{0,1:T(2,128)}, u32[]{:S(2)}) copy-start(s32[9,2]{0,1:T(2,128)} %param.14) | copy-start | bytes 220
  7.2 29.6 %copy-start.11 = (f32[9]{0:T(128)S(1)}, f32[9]{0:T(128)}, u32[]{:S(2)}) copy-start(f32[9]{0:T(128)} %param.15) | copy-start | bytes 112
  25.1 0.7 copy-start.7
  25.8 29.8 %collective-permute-start.2 = (f32[4,1024]{1,0:T(4,128)S(1)}, f32[4,1024]{1,0:T(4,128)S(1)}, u32[]{:S(2)}, u32[]{:S(2)}) collective-permute-start(f32[4,1024]{1,0:T(4,128)S(1)} %get-tuple-element.28), channel_id=1, source_target_pairs={{0,2},{2,4},{4,6},{1,3},{3,5},{5,7},{8,10},{10,12},{12,14},{9,11},... | collective-permute-start | bytes 49160 | tf_op jit(solution)/shard_map/ppermute | solution.py:17
  29.0 26.6 %collective-permute-start.3 = (f32[4,1024]{1,0:T(4,128)S(1)}, f32[4,1024]{1,0:T(4,128)S(1)}, u32[]{:S(2)}, u32[]{:S(2)}) collective-permute-start(f32[4,1024]{1,0:T(4,128)S(1)} %get-tuple-element.29), channel_id=1, source_target_pairs={{2,0},{4,2},{6,4},{3,1},{5,3},{7,5},{10,8},{12,10},{14,12},{11,9},... | collective-permute-start | bytes 49160 | tf_op jit(solution)/shard_map/ppermute | solution.py:18
  31.5 12.3 %collective-permute-start = (f32[12,7,1024]{2,1,0:T(8,128)S(1)}, f32[12,7,1024]{2,1,0:T(8,128)S(1)}, u32[]{:S(2)}, u32[]{:S(2)}) collective-permute-start(f32[12,7,1024]{2,1,0:T(8,128)S(1)} %get-tuple-element.24), channel_id=1, source_target_pairs={{0,2},{2,4},{4,6},{1,3},{3,5},{5,7},{8,10},{10,12},{12,14},{9,11},... | collective-permute-start | bytes 1032200 | tf_op jit(solution)/shard_map/ppermute | solution.py:17
  35.5 12.2 %collective-permute-start.1 = (f32[12,7,1024]{2,1,0:T(8,128)S(1)}, f32[12,7,1024]{2,1,0:T(8,128)S(1)}, u32[]{:S(2)}, u32[]{:S(2)}) collective-permute-start(f32[12,7,1024]{2,1,0:T(8,128)S(1)} %get-tuple-element.25), channel_id=1, source_target_pairs={{2,0},{4,2},{6,4},{3,1},{5,3},{7,5},{10,8},{12,10},{14,12},{11,9},... | collective-permute-start | bytes 1032200 | tf_op jit(solution)/shard_map/ppermute | solution.py:18
  53.6 0.7 copy-start.6
  53.6 1.7 copy-start.2
  54.3 0.7 copy-start.5
  54.6 60.1 %copy-start.1 = (f32[10,40,1024]{2,1,0:T(8,128)}, f32[10,40,1024]{2,1,0:T(8,128)S(1)}, u32[]{:S(2)}) copy-start(f32[10,40,1024]{2,1,0:T(8,128)S(1)} %subtract_multiply_fusion) | copy-start | bytes 4915204
  54.6 57.4 %all-reduce.12.cloned.1.call-start = ((), (), s32[]{:S(2)}) async-start(), calls=%async_computation.2 | async-start | bytes 327680 | tf_op jit(solution)/shard_map/psum | solution.py:67
  55.4 144.6 %reduce-scatter.3.cloned.1.call-start = ((), (), s32[]{:S(2)}) async-start(), calls=%async_computation.3 | async-start | bytes 147456 | tf_op jit(solution)/shard_map/reduce_scatter | solution.py:101
  166.6 142.6 %reduce-scatter.5.cloned.1.call-start = ((), (), s32[]{:S(2)}) async-start(), calls=%async_computation.4 | async-start | bytes 147456 | tf_op jit(solution)/shard_map/reduce_scatter | solution.py:103
  215.6 4.6 %collective-permute-start.4 = (f32[4,1024]{1,0:T(4,128)S(1)}, f32[4,1024]{1,0:T(4,128)S(1)}, u32[]{:S(2)}, u32[]{:S(2)}) collective-permute-start(f32[4,1024]{1,0:T(4,128)S(1)} %get-tuple-element.26), channel_id=1, source_target_pairs={{0,2},{2,4},{4,6},{1,3},{3,5},{5,7},{8,10},{10,12},{12,14},{9,11},... | collective-permute-start | bytes 49160 | tf_op jit(solution)/shard_map/ppermute | solution.py:17
  218.7 4.9 %collective-permute-start.5 = (f32[4,1024]{1,0:T(4,128)S(1)}, f32[4,1024]{1,0:T(4,128)S(1)}, u32[]{:S(2)}, u32[]{:S(2)}) collective-permute-start(f32[4,1024]{1,0:T(4,128)S(1)} %get-tuple-element.27), channel_id=1, source_target_pairs={{2,0},{4,2},{6,4},{3,1},{5,3},{7,5},{10,8},{12,10},{14,12},{11,9},... | collective-permute-start | bytes 49160 | tf_op jit(solution)/shard_map/ppermute | solution.py:18
  251.5 57.7 %copy-start.9 = (f32[32,128]{1,0:T(8,128)S(1)}, f32[32,128]{1,0:T(8,128)}, u32[]{:S(2)}) copy-start(f32[32,128]{1,0:T(8,128)} %reduce-scatter.3.cloned.1.call-done) | copy-start | bytes 49156
  310.0 17.6 %copy-start.8 = (f32[32,128]{1,0:T(8,128)}, f32[32,128]{1,0:T(8,128)S(1)}, u32[]{:S(2)}) copy-start(f32[32,128]{1,0:T(8,128)S(1)} %multiply_add_fusion) | copy-start | bytes 49156
Sparse Core Ops, SparseCore 0:
  59.1 52.8 all-reduce.11
  166.7 33.1 reduce-scatter.2
  277.4 31.8 reduce-scatter.4
where the time goes:
time: 336 us; the launch traced here: 334 us
  waiting for transfers between devices  132 us (39%)
  other arithmetic  123 us (37%)
  blocking collectives  45 us (13%)
  starting transfers between devices  14.7 us (4%)
  between operations  14.1 us (4%)
  local copies, waits for them, and re-layouts  4.14 us (1%)
    psum x1, waiting for transfers between devices, on_device(): mean = lax.psum(own, GROUP) / groups  55.5 us
    mul x3, other arithmetic, apply(): z = spread_out(dev * h[None], taps, -1) * inside  54 us
    reduce_sum x2, other arithmetic, apply(): return jnp.sum(dev[:, reach:reach + rows] * y, axis=0) * -STEP_SIZE  50.1 us
    reduce_scatter x1, waiting for transfers between devices, on_device(): lax.psum_scatter(apply(gathered(-dense_wi)), GROUP, scatter_dimension=1,...  33.3 us
    reduce_scatter x1, waiting for transfers between devices, on_device(): lax.psum_scatter(apply(gathered(g1)), GROUP, scatter_dimension=1, tiled=T...  32 us
    all_gather x2, blocking collectives, gathered(): lax.all_gather(block, GROUP, axis=1, tiled=True)  30.1 us
    all_gather x1, blocking collectives, on_device(): full = lax.all_gather(block, GROUP, axis=1, tiled=True)  14.9 us
    ppermute x3, starting transfers between devices, halo(): above = lax.ppermute(tail, axis, [(i, i + 1) for i in range(count - 1)])  10.3 us
  transfers between devices with their start and end apart: 9, of which 6 were waited for; matrix products, arithmetic and copies ran while one was open for 3% of the time, Pallas kernels for 0%

commit v1 on v0

--- a/solution.py
+++ b/solution.py
@@ -8,6 +8,11 @@
 FSTEPS = 3
 STEP_SIZE = 0.25
 GROUP = ("member", "grp")
+
+
+def add_all(block, name):
+    parts = lax.all_gather(block, name)
+    return jnp.sum(parts, axis=0)
 
 
 def halo(cells, axis, width, dim):
@@ -64,7 +69,7 @@
         q = upwind(q, cx[lo:hi], cy[lo:hi])
     fields = q[:, reach : reach + rows]
     own = jnp.sum(q, axis=0) / n
-    mean = lax.psum(own, GROUP) / groups
+    mean = add_all(own, GROUP) / groups
     dev = (q - own[None]) / math.sqrt(total - 1)
     shift = (own - mean) * math.sqrt(n / (total - 1))
     ones = jnp.full_like(own, 1.0 / math.sqrt(groups))

time: 336 us -> 281 us (0.84)
  waiting for transfers between devices: 132 us -> 78.6 us
    psum x1 -> x0, waiting for transfers between devices: 55.5 us -> none  [on_device(): mean = lax.psum(own, GROUP) / groups]
  transfers between devices with their start and end apart: 9 -> 9, of which waited for: 6 -> 6; matrix products, arithmetic and copies ran while one was open for 3% -> 2% of each run, Pallas kernels for 0% -> 0%
where the time goes in v1:
time: 281 us; the launch traced here: 280 us
  other arithmetic  124 us (44%)
  waiting for transfers between devices  78.6 us (28%)
  blocking collectives  45.4 us (16%)
  starting transfers between devices  14.7 us (5%)
  between operations  14.2 us (5%)
    mul x3, other arithmetic, apply(): z = spread_out(dev * h[None], taps, -1) * inside  53.9 us
    reduce_sum x2, other arithmetic, apply(): return jnp.sum(dev[:, reach:reach + rows] * y, axis=0) * -STEP_SIZE  50 us
    reduce_scatter x1, waiting for transfers between devices, on_device(): lax.psum_scatter(apply(gathered(-dense_wi)), GROUP, scatter_dimension=1,...  32.9 us
    reduce_scatter x1, waiting for transfers between devices, on_device(): lax.psum_scatter(apply(gathered(g1)), GROUP, scatter_dimension=1, tiled=T...  32 us
    all_gather x2, blocking collectives, gathered(): lax.all_gather(block, GROUP, axis=1, tiled=True)  30.5 us
    all_gather x1, blocking collectives, on_device(): full = lax.all_gather(block, GROUP, axis=1, tiled=True)  14.9 us
    ppermute x3, starting transfers between devices, halo(): above = lax.ppermute(tail, axis, [(i, i + 1) for i in range(count - 1)])  10.3 us
    ppermute x3, waiting for transfers between devices, halo(): below = lax.ppermute(head, axis, [(i + 1, i) for i in range(count - 1)])  7.98 us
  transfers between devices with their start and end apart: 9, of which 6 were waited for; matrix products, arithmetic and copies ran while one was open for 2% of the time, Pallas kernels for 0%

profile of v1, /device:TPU:1, one launch (start us, length us, event | category | flops | bytes accessed | tf_op | source)
XLA Modules:
  0.0 280.0 jit_solution(2505273539901154068)
XLA Ops:
  7.3 1.3 pad_maximum_fusion.3
  8.6 4.0 %collective-permute-start = (f32[12,7,1024]{2,1,0:T(8,128)S(1)}, f32[12,7,1024]{2,1,0:T(8,128)S(1)}, u32[]{:S(2)}, u32[]{:S(2)}) collective-permute-start(f32[12,7,1024]{2,1,0:T(8,128)S(1)} %get-tuple-element.24), channel_id=1, source_target_pairs={{0,2},{2,4},{4,6},{1,3},{3,5},{5,7},{8,10},{10,12},{12,14},{9,11},... | collective-permute-start | bytes 1032200 | tf_op jit(solution)/shard_map/ppermute | solution.py:22
  12.6 1.3 collective-permute-start.1
  14.0 0.7 fusion.218
  14.7 5.7 %collective-permute-done = f32[12,7,1024]{2,1,0:T(8,128)S(1)} collective-permute-done((f32[12,7,1024]{2,1,0:T(8,128)S(1)}, f32[12,7,1024]{2,1,0:T(8,128)S(1)}, u32[]{:S(2)}, u32[]{:S(2)}) %collective-permute-start) | collective-permute-done | bytes 344096 | tf_op jit(solution)/shard_map/ppermute | solution.py:22
  20.4 3.9 %collective-permute-done.1 = f32[12,7,1024]{2,1,0:T(8,128)S(1)} collective-permute-done((f32[12,7,1024]{2,1,0:T(8,128)S(1)}, f32[12,7,1024]{2,1,0:T(8,128)S(1)}, u32[]{:S(2)}, u32[]{:S(2)}) %collective-permute-start.1) | collective-permute-done | bytes 344096 | tf_op jit(solution)/shard_map/ppermute | solution.py:23
  24.3 0.4 pad_maximum_fusion
  24.7 0.4 slice.749
  25.0 0.1 maximum_bitcast_fusion.3
  25.2 1.5 fusion.93
  26.7 0.4 slice.752
  27.1 0.1 maximum_bitcast_fusion.1
  27.2 1.5 fusion.99
  28.7 0.3 slice.755
  29.2 1.1 fusion.223
  30.3 0.7 broadcast_multiply_fusion.2
  31.1 0.4 fusion.212
  31.6 15.7 %all_gather.14 = f32[32,1024]{1,0:T(8,128)S(1)} all-gather(f32[32,128]{1,0:T(8,128)S(1)} %slice_negate_fusion), channel_id=1, replica_groups=mesh['member'=4,'tile'=4,'grp'=2] {'member','grp'}, dimensions={1}, use_global_device_ids=true | all-gather | bytes 147456 | tf_op jit(solution)/shard_map/all_gather | solution.py:104
  47.2 3.1 %collective-permute-start.2 = (f32[4,1024]{1,0:T(4,128)S(1)}, f32[4,1024]{1,0:T(4,128)S(1)}, u32[]{:S(2)}, u32[]{:S(2)}) collective-permute-start(f32[4,1024]{1,0:T(4,128)S(1)} %get-tuple-element.28), channel_id=1, source_target_pairs={{0,2},{2,4},{4,6},{1,3},{3,5},{5,7},{8,10},{10,12},{12,14},{9,11},... | collective-permute-start | bytes 49160 | tf_op jit(solution)/shard_map/ppermute | solution.py:22
  50.3 1.5 collective-permute-start.3
  51.8 0.6 reduce_sum.57
  52.5 0.1 select_reduce_fusion
  52.6 0.7 broadcast_divide_fusion
  53.3 0.7 fusion.228
  53.9 0.7 fusion.227
  54.7 0.1 pad.58.clone
  54.7 0.8 collective-permute-done.3
  55.6 0.7 pad_maximum_fusion.10
  56.3 1.2 subtract_multiply_fusion
  57.5 2.0 reduce_sum.55
  59.6 1.7 maximum_maximum_fusion
  61.2 26.1 %fusion.44 = f32[12,36,1024]{2,1,0:T(8,128)S(1)} fusion(f32[12,40,1024]{2,1,0:T(8,128)S(1)} %get-tuple-element.23, f32[36]{0:T(128)S(1)} %and_convert_fusion, f32[]{:T(128)} %bitcast.45, f32[]{:T(128)} %bitcast.44, f32[]{:T(128)} %bitcast.43, f32[]{:T(128)} %bitcast.42, f32[]{:T(128)} %bitcast.41, f32[]{:T(128)} %bitcast.40, f32[]{:T(128)} %bitcast.39, ...), kind=kLoop, calls=%fused_computation.129 | loop fusion | flops 22118400 | bytes 13566564 | tf_op jit(solution)/shard_map/mul | solution.py:86
  87.3 25.0 %fusion.164 = f32[32,1024]{1,0:T(8,128)S(1)} fusion(f32[12,36,1024]{2,1,0:T(8,128)S(1)} %fusion.44, f32[12,40,1024]{2,1,0:T(8,128)} %get-tuple-element.22, f32[]{:T(128)} %bitcast.45, f32[]{:T(128)} %bitcast.44, f32[]{:T(128)} %bitcast.43, f32[]{:T(128)} %bitcast.42, f32[]{:T(128)} %bitcast.41, f32[]{:T(128)} %bitcast.40, f32[]{:T(128)} %bitcast.39, ...), kind=kLoop, calls=%fused_computation.269 | loop fusion | flops 20021248 | bytes 11534436 | tf_op jit(solution)/shard_map/reduce_sum | solution.py:88
  112.3 0.7 broadcast_multiply_fusion.4
  113.0 32.9 %reduce-scatter.3.cloned.1.call-done = f32[32,128]{1,0:T(8,128)} async-done(((f32[32,1024]{1,0:T(8,128)}), f32[32,128]{1,0:T(8,128)}) %reduce-scatter.3.cloned.1.call-update) | async-done | bytes 16400 | tf_op jit(solution)/shard_map/reduce_scatter | solution.py:106
  145.9 0.7 fusion.219
  146.6 14.9 %all_gather.15 = f32[32,1024]{1,0:T(8,128)S(1)} all-gather(f32[32,128]{1,0:T(8,128)S(1)} %fusion.219), channel_id=1, replica_groups=mesh['member'=4,'tile'=4,'grp'=2] {'member','grp'}, dimensions={1}, use_global_device_ids=true | all-gather | bytes 147456 | tf_op jit(solution)/shard_map/all_gather | solution.py:104
  161.5 3.1 %collective-permute-start.4 = (f32[4,1024]{1,0:T(4,128)S(1)}, f32[4,1024]{1,0:T(4,128)S(1)}, u32[]{:S(2)}, u32[]{:S(2)}) collective-permute-start(f32[4,1024]{1,0:T(4,128)S(1)} %get-tuple-element.26), channel_id=1, source_target_pairs={{0,2},{2,4},{4,6},{1,3},{3,5},{5,7},{8,10},{10,12},{12,14},{9,11},... | collective-permute-start | bytes 49160 | tf_op jit(solution)/shard_map/ppermute | solution.py:22
  164.7 1.5 collective-permute-start.5
  166.2 3.3 %collective-permute-done.5 = f32[4,1024]{1,0:T(4,128)S(1)} collective-permute-done((f32[4,1024]{1,0:T(4,128)S(1)}, f32[4,1024]{1,0:T(4,128)S(1)}, u32[]{:S(2)}, u32[]{:S(2)}) %collective-permute-start.5) | collective-permute-done | bytes 16416 | tf_op jit(solution)/shard_map/ppermute | solution.py:23
  169.5 1.7 broadcast_multiply_fusion
  171.3 26.1 %fusion.89 = f32[12,36,1024]{2,1,0:T(8,128)S(1)} fusion(f32[12,40,1024]{2,1,0:T(8,128)S(1)} %broadcast_multiply_fusion, f32[36]{0:T(128)S(1)} %and_convert_fusion, f32[]{:T(128)} %bitcast.45, f32[]{:T(128)} %bitcast.44, f32[]{:T(128)} %bitcast.43, f32[]{:T(128)} %bitcast.42, f32[]{:T(128)} %bitcast.41, f32[]{:T(128)} %bitcast.40, f32[]{:T(128)} %bitcast.39, ...), kind=kLoop, calls=%fused_computation.174 | loop fusion | flops 22118400 | bytes 13566564 | tf_op jit(solution)/shard_map/mul | solution.py:86
  197.4 25.0 %fusion.210 = f32[32,1024]{1,0:T(8,128)S(1)} fusion(f32[12,36,1024]{2,1,0:T(8,128)S(1)} %fusion.89, f32[12,40,1024]{2,1,0:T(8,128)} %get-tuple-element.22, f32[]{:T(128)} %bitcast.45, f32[]{:T(128)} %bitcast.44, f32[]{:T(128)} %bitcast.43, f32[]{:T(128)} %bitcast.42, f32[]{:T(128)} %bitcast.41, f32[]{:T(128)} %bitcast.40, f32[]{:T(128)} %bitcast.39, ...), kind=kLoop, calls=%fused_computation.315 | loop fusion | flops 20021248 | bytes 11534436 | tf_op jit(solution)/shard_map/reduce_sum | solution.py:88
  222.4 0.7 broadcast_multiply_fusion.3
  223.1 32.0 %reduce-scatter.5.cloned.1.call-done = f32[32,128]{1,0:T(8,128)} async-done(((f32[32,1024]{1,0:T(8,128)}), f32[32,128]{1,0:T(8,128)}) %reduce-scatter.5.cloned.1.call-update) | async-done | bytes 16400 | tf_op jit(solution)/shard_map/reduce_scatter | solution.py:108
  255.1 0.7 multiply_add_fusion
  255.8 14.9 %all_gather.16 = f32[32,1024]{1,0:T(8,128)S(1)} all-gather(f32[32,128]{1,0:T(8,128)S(1)} %multiply_add_fusion), channel_id=1, replica_groups=mesh['member'=4,'tile'=4,'grp'=2] {'member','grp'}, dimensions={1}, use_global_device_ids=true | all-gather | bytes 147456 | tf_op jit(solution)/shard_map/all_gather | solution.py:110
  270.7 2.7 slice_add_fusion
  (54 shorter events, 0.6 us)
Async XLA Ops:
  7.2 17.1 %copy-start = (f32[10,32,1024]{2,1,0:T(8,128)S(1)}, f32[10,32,1024]{2,1,0:T(8,128)}, u32[]{:S(2)}) copy-start(f32[10,32,1024]{2,1,0:T(8,128)} %param.8) | copy-start | bytes 3932164
  7.2 17.1 %copy-start.3 = (f32[32,1024]{1,0:T(8,128)S(1)}, f32[32,1024]{1,0:T(8,128)}, u32[]{:S(2)}) copy-start(f32[32,1024]{1,0:T(8,128)} %param.10) | copy-start | bytes 393220
  7.2 17.1 %copy-start.4 = (f32[32,1024]{1,0:T(8,128)S(1)}, f32[32,1024]{1,0:T(8,128)}, u32[]{:S(2)}) copy-start(f32[32,1024]{1,0:T(8,128)} %param.9) | copy-start | bytes 393220
  7.2 6.8 %copy-start.10 = (f32[1,1,1024]{2,1,0:T(1,128)S(1)}, f32[1,1,1024]{2,1,0:T(1,128)}, u32[]{:S(2)}) copy-start(f32[1,1,1024]{2,1,0:T(1,128)} %param.13) | copy-start | bytes 12292
  7.2 6.8 %copy-start.11 = (f32[1,1,1024]{2,1,0:T(1,128)S(1)}, f32[1,1,1024]{2,1,0:T(1,128)}, u32[]{:S(2)}) copy-start(f32[1,1,1024]{2,1,0:T(1,128)} %param.12) | copy-start | bytes 12292
  7.2 6.8 %copy-start.12 = (s32[1,1,1024]{2,1,0:T(1,128)S(1)}, s32[1,1,1024]{2,1,0:T(1,128)}, u32[]{:S(2)}) copy-start(s32[1,1,1024]{2,1,0:T(1,128)} %param.11) | copy-start | bytes 12292
  7.2 50.3 %all-gather.3.cloned.1.call-start = ((), (), s32[]{:S(2)}) async-start(), calls=%async_computation.4 | async-start | bytes 1474560 | tf_op jit(solution)/shard_map/all_gather | solution.py:14
  8.6 11.8 %collective-permute-start = (f32[12,7,1024]{2,1,0:T(8,128)S(1)}, f32[12,7,1024]{2,1,0:T(8,128)S(1)}, u32[]{:S(2)}, u32[]{:S(2)}) collective-permute-start(f32[12,7,1024]{2,1,0:T(8,128)S(1)} %get-tuple-element.24), channel_id=1, source_target_pairs={{0,2},{2,4},{4,6},{1,3},{3,5},{5,7},{8,10},{10,12},{12,14},{9,11},... | collective-permute-start | bytes 1032200 | tf_op jit(solution)/shard_map/ppermute | solution.py:22
  12.6 11.6 %collective-permute-start.1 = (f32[12,7,1024]{2,1,0:T(8,128)S(1)}, f32[12,7,1024]{2,1,0:T(8,128)S(1)}, u32[]{:S(2)}, u32[]{:S(2)}) collective-permute-start(f32[12,7,1024]{2,1,0:T(8,128)S(1)} %get-tuple-element.25), channel_id=1, source_target_pairs={{2,0},{4,2},{6,4},{3,1},{5,3},{7,5},{10,8},{12,10},{14,12},{11,9},... | collective-permute-start | bytes 1032200 | tf_op jit(solution)/shard_map/ppermute | solution.py:23
  29.1 2.0 copy-start.6
  29.1 2.0 copy-start.7
  29.1 22.7 %copy-start.14 = (f32[9]{0:T(128)S(1)}, f32[9]{0:T(128)}, u32[]{:S(2)}) copy-start(f32[9]{0:T(128)} %param.15) | copy-start | bytes 112
  29.1 23.3 %copy-start.13 = (s32[9,2]{0,1:T(2,128)S(1)}, s32[9,2]{0,1:T(2,128)}, u32[]{:S(2)}) copy-start(s32[9,2]{0,1:T(2,128)} %param.14) | copy-start | bytes 220
  30.3 27.2 %copy-start.2 = (f32[10,40,1024]{2,1,0:T(8,128)}, f32[10,40,1024]{2,1,0:T(8,128)S(1)}, u32[]{:S(2)}) copy-start(f32[10,40,1024]{2,1,0:T(8,128)S(1)} %get-tuple-element.3) | copy-start | bytes 4915204
  31.0 114.9 %reduce-scatter.3.cloned.1.call-start = ((), (), s32[]{:S(2)}) async-start(), calls=%async_computation.2 | async-start | bytes 147456 | tf_op jit(solution)/shard_map/reduce_scatter | solution.py:106
  47.2 7.5 %collective-permute-start.2 = (f32[4,1024]{1,0:T(4,128)S(1)}, f32[4,1024]{1,0:T(4,128)S(1)}, u32[]{:S(2)}, u32[]{:S(2)}) collective-permute-start(f32[4,1024]{1,0:T(4,128)S(1)} %get-tuple-element.28), channel_id=1, source_target_pairs={{0,2},{2,4},{4,6},{1,3},{3,5},{5,7},{8,10},{10,12},{12,14},{9,11},... | collective-permute-start | bytes 49160 | tf_op jit(solution)/shard_map/ppermute | solution.py:22
  50.3 5.2 %collective-permute-start.3 = (f32[4,1024]{1,0:T(4,128)S(1)}, f32[4,1024]{1,0:T(4,128)S(1)}, u32[]{:S(2)}, u32[]{:S(2)}) collective-permute-start(f32[4,1024]{1,0:T(4,128)S(1)} %get-tuple-element.29), channel_id=1, source_target_pairs={{2,0},{4,2},{6,4},{3,1},{5,3},{7,5},{10,8},{12,10},{14,12},{11,9},... | collective-permute-start | bytes 49160 | tf_op jit(solution)/shard_map/ppermute | solution.py:23
  57.5 3.8 %copy-start.1 = (f32[10,40,1024]{2,1,0:T(8,128)}, f32[10,40,1024]{2,1,0:T(8,128)S(1)}, u32[]{:S(2)}) copy-start(f32[10,40,1024]{2,1,0:T(8,128)S(1)} %subtract_multiply_fusion) | copy-start | bytes 4915204
  57.5 2.0 copy-start.5
  113.0 142.1 %reduce-scatter.5.cloned.1.call-start = ((), (), s32[]{:S(2)}) async-start(), calls=%async_computation.3 | async-start | bytes 147456 | tf_op jit(solution)/shard_map/reduce_scatter | solution.py:108
  161.5 4.7 %collective-permute-start.4 = (f32[4,1024]{1,0:T(4,128)S(1)}, f32[4,1024]{1,0:T(4,128)S(1)}, u32[]{:S(2)}, u32[]{:S(2)}) collective-permute-start(f32[4,1024]{1,0:T(4,128)S(1)} %get-tuple-element.26), channel_id=1, source_target_pairs={{0,2},{2,4},{4,6},{1,3},{3,5},{5,7},{8,10},{10,12},{12,14},{9,11},... | collective-permute-start | bytes 49160 | tf_op jit(solution)/shard_map/ppermute | solution.py:22
  164.7 4.8 %collective-permute-start.5 = (f32[4,1024]{1,0:T(4,128)S(1)}, f32[4,1024]{1,0:T(4,128)S(1)}, u32[]{:S(2)}, u32[]{:S(2)}) collective-permute-start(f32[4,1024]{1,0:T(4,128)S(1)} %get-tuple-element.27), channel_id=1, source_target_pairs={{2,0},{4,2},{6,4},{3,1},{5,3},{7,5},{10,8},{12,10},{14,12},{11,9},... | collective-permute-start | bytes 49160 | tf_op jit(solution)/shard_map/ppermute | solution.py:23
  197.4 57.7 %copy-start.9 = (f32[32,128]{1,0:T(8,128)S(1)}, f32[32,128]{1,0:T(8,128)}, u32[]{:S(2)}) copy-start(f32[32,128]{1,0:T(8,128)} %reduce-scatter.3.cloned.1.call-done) | copy-start | bytes 49156
  255.8 17.6 %copy-start.8 = (f32[32,128]{1,0:T(8,128)}, f32[32,128]{1,0:T(8,128)S(1)}, u32[]{:S(2)}) copy-start(f32[32,128]{1,0:T(8,128)S(1)} %multiply_add_fusion) | copy-start | bytes 49156
Sparse Core Ops, SparseCore 0:
  31.2 26.3 all-gather.2
  113.1 32.7 reduce-scatter.2
  223.2 31.8 reduce-scatter.4
